TPU v7x, 512 devices: a whole 4x8x8 slice. The times are simulated.
512 devices in a mesh: space: 64 (over x, y, z_lo), mode: 8 (over z_hi, core).
Axes of the slice: x: 4, y: 8, z: 8 (z_hi: 4, z_lo: 2; z = z_hi * 2 + z_lo), core: 2. Of those that a mesh axis runs over, the one named last changes fastest.
Arguments:
- state: float32 [858, 65536], P(None, ('space', 'mode')), may hold values from -6 to 6
- tensor: bfloat16 [64, 286, 858], P('mode'), may hold values from -0.01171875 to 0.01171875
- table: int32 [286, 3], replicated, may hold values from 0 to 10, as said below
- thermal: float32 [3], replicated, may hold values from 0.5 to 2
- output_mode_row: int32 [64], replicated, may hold values from 0 to 857, as said below
Outputs:
- updated: float32 [858, 65536], P(None, ('space', 'mode'))
- collision: float32 [64, 65536], P('mode', 'space')
Inputs may be any that keep to these rules, and one draw needn't show every extreme that they name: `table`: each row holds the three indices of one multi-index of total degree at most 10; every such multi-index is in exactly one row. `output_mode_row`: all entries are different.
All inputs are finite; a program needn't handle non-finite values.
Results may differ from a plain program's by a relative error of at most 0.004.
Values may be sent and summed in bfloat16 or wider, within the bound.
A program may use at most 64 MiB of HBM per device.

v0:
```python
import jax
import jax.numpy as jnp
from jax import lax
from jax.sharding import PartitionSpec as P

CLASSES = 3
MODES = 286
wave_bound = 5.2
courant = 0.09
collision_update = 0.1


def extended_2(x, sides, width):
    for axis, dim in sides:
        size, length = (lax.axis_size(axis), x.shape[dim])
        up = [(i, (i + 1) % size) for i in range(size)]
        down = [(j, i) for i, j in up]
        last = lax.slice_in_dim(x, length - width, length, axis=dim)
        first = lax.slice_in_dim(x, 0, width, axis=dim)
        before = lax.ppermute(last, axis, up)
        after = lax.ppermute(first, axis, down)
        x = jnp.concatenate([before, x, after], axis=dim)
    return x


def advection_matrix(table):
    codes = table[:, 0] * 144 + table[:, 1] * 12 + table[:, 2]
    along = table[:, 0].astype(jnp.float32)
    lower = (codes[None, :] == codes[:, None] - 144).astype(jnp.float32)
    higher = (codes[None, :] == codes[:, None] + 144).astype(jnp.float32)
    return jnp.sqrt(along)[:, None] * lower + jnp.sqrt(along + 1.0)[:, None] * higher


def upwind_transport(extended, state, matrix, thermal):
    blocks = extended.reshape(CLASSES, MODES, -1)
    state_after_collision = jnp.einsum(
        "ab,cbx->cax", matrix, blocks, precision=lax.Precision.HIGHEST
    )
    speed = thermal[:, None, None]
    flux = 0.5 * speed * (
        state_after_collision[:, :, :-1] + state_after_collision[:, :, 1:]
    ) - 0.5 * wave_bound * speed * (blocks[:, :, 1:] - blocks[:, :, :-1])
    change = (flux[:, :, 1:] - flux[:, :, :-1]).reshape(CLASSES * MODES, -1)
    return state - courant * change


def shards(state, tensor, table, thermal, output_mode_row):
    per_device = tensor.shape[0]
    own_modes = lax.dynamic_slice_in_dim(
        output_mode_row, lax.axis_index("mode") * per_device, per_device
    )
    mode_selector = ((own_modes // MODES)[:, None] == jnp.arange(CLASSES)[None, :]).astype(
        jnp.float32
    )
    flat = tensor.reshape(per_device * MODES, CLASSES * MODES)
    matrix = advection_matrix(table)
    piece = lax.all_gather(state.astype(jnp.bfloat16), "mode", axis=1, tiled=True)
    width = piece.shape[1]
    product = jnp.dot(flat, piece, preferred_element_type=jnp.float32).reshape(
        per_device, MODES, width
    )
    first = jnp.einsum(
        "oc,cix->oix", mode_selector, piece.reshape(CLASSES, MODES, width).astype(jnp.float32)
    )
    collision = jnp.sum(first * product, axis=1)
    extended = extended_2(state, ((("space", "mode"), 1),), 1)
    advected_state = upwind_transport(extended, state, matrix, thermal)
    own_terms = lax.all_to_all(
        collision.astype(jnp.bfloat16), "mode", split_axis=1, concat_axis=0, tiled=True
    ).astype(collision.dtype)
    placing = (jnp.arange(CLASSES * MODES)[:, None] == output_mode_row[None, :]).astype(jnp.float32)
    collision_increment = jnp.dot(
        placing, own_terms, precision=lax.Precision.HIGHEST, preferred_element_type=jnp.float32
    )
    updated = advected_state + collision_update * collision_increment
    return (updated, collision)


def solution(mesh):
    in_specs = (P(None, ("space", "mode")), P("mode", None, None), P(), P(), P())
    out_specs = (P(None, ("space", "mode")), P("mode", "space"))
    return jax.shard_map(shards, mesh=mesh, in_specs=in_specs, out_specs=out_specs, check_vma=False)
```

profile of v0, /device:TPU:4, one launch (start us, length us, event | category | flops | bytes accessed | tf_op | source)
XLA Modules:
  0.0 88.0 jit_solution(16369945874256971813)
XLA Ops:
  7.2 0.0 all-gather.2.cloned.1.call-start
  7.2 1.7 %convert_element_type.22 = bf16[858,128]{1,0:T(8,128)(2,1)} convert(f32[858,128]{1,0:T(8,128)} %param.5) | non-fusion elementwise | flops 109824 | bytes 658944 | tf_op jit(solution)/shard_map/convert_element_type | solution.py:57
  8.9 0.0 all-gather.2.cloned.1.call-update
  9.0 1.3 %fusion.26 = (f32[858,1]{1,0:T(8,128)S(1)}, f32[858,1]{1,0:T(8,128)S(1)}) fusion(f32[858,128]{1,0:T(8,128)} %param.5), kind=kLoop, calls=%fused_computation.42 | loop fusion | bytes 13728 | tf_op jit(solution)/shard_map/slice | solution.py:18
  10.3 1.9 %collective-permute-start = (f32[858,1]{1,0:T(8,128)S(1)}, f32[858,1]{1,0:T(8,128)S(1)}, u32[]{:S(2)}, u32[]{:S(2)}) collective-permute-start(f32[858,1]{1,0:T(8,128)S(1)} %get-tuple-element.9), channel_id=1, source_target_pairs={{0,1},{1,2},{2,3},{3,4},{4,5},{5,6},{6,7},{7,8},{8,9},{9,10},{10,1... | collective-permute-start | bytes 10304 | tf_op jit(solution)/shard_map/ppermute | solution.py:20
  12.2 13.3 %collective-permute-start.1 = (f32[858,1]{1,0:T(8,128)S(1)}, f32[858,1]{1,0:T(8,128)S(1)}, u32[]{:S(2)}, u32[]{:S(2)}) collective-permute-start(f32[858,1]{1,0:T(8,128)S(1)} %get-tuple-element.10), channel_id=1, source_target_pairs={{1,0},{2,1},{3,2},{4,3},{5,4},{6,5},{7,6},{8,7},{9,8},{10,9},{11,1... | collective-permute-start | bytes 10304 | tf_op jit(solution)/shard_map/ppermute | solution.py:21
  25.5 0.7 sqrt_reduce_fusion.1
  26.2 0.8 add_reduce_fusion.1
  27.0 0.7 broadcast_multiply_fusion.1
  27.7 0.7 and_select_fusion
  28.4 3.0 %collective-permute-done = f32[858,1]{1,0:T(8,128)S(1)} collective-permute-done((f32[858,1]{1,0:T(8,128)S(1)}, f32[858,1]{1,0:T(8,128)S(1)}, u32[]{:S(2)}, u32[]{:S(2)}) %collective-permute-start) | collective-permute-done | bytes 3464 | tf_op jit(solution)/shard_map/ppermute | solution.py:20
  31.4 1.4 %collective-permute-done.1 = f32[858,1]{1,0:T(8,128)S(1)} collective-permute-done((f32[858,1]{1,0:T(8,128)S(1)}, f32[858,1]{1,0:T(8,128)S(1)}, u32[]{:S(2)}, u32[]{:S(2)}) %collective-permute-start.1) | collective-permute-done | bytes 3464 | tf_op jit(solution)/shard_map/ppermute | solution.py:21
  32.8 1.4 %pad_maximum_fusion = f32[858,130]{1,0:T(8,128)S(1)} fusion(f32[858,1]{1,0:T(8,128)S(1)} %collective-permute-done.1, f32[858,128]{1,0:T(8,128)} %param.5, f32[858,1]{1,0:T(8,128)S(1)} %collective-permute-done), kind=kLoop, calls=%fused_computation.7 | loop fusion | flops 223080 | bytes 892320 | tf_op jit(solution)/shard_map/concatenate | solution.py:22
  34.2 0.1 reshape.57
  34.3 0.3 fusion.25
  34.6 0.3 copy.22
  34.9 0.3 copy.21
  35.3 3.6 %convolution_bitcast_fusion = f32[3,286,130]{1,2,0:T(8,128)S(1)} fusion(f32[3,286,130]{2,1,0:T(8,128)S(1)} %reshape.57, f32[286]{0:T(512)S(1)} %get-tuple-element.3, f32[286]{0:T(512)S(1)} %get-tuple-element.2, s32[286]{0:T(512)S(1)} %get-tuple-element.6, s32[286]{0:T(512)S(1)} %get-tuple-element.5, s32[286]{0:T(512)S(1)} %get-tuple-element.4), kind=kOutput, calls=%fused_computation.4 | convolution fusion | flops 383214272 | bytes 898040 | tf_op jit(solution)/shard_map/ab,cbx->cax/dot_general | solution.py:36
  38.9 0.2 fusion.5
  39.1 16.5 %all-gather.2.cloned.1.call-done = bf16[858,1024]{1,0:T(8,128)(2,1)} async-done(((bf16[858,128]{1,0:T(8,128)(2,1)}), bf16[858,1024]{1,0:T(8,128)(2,1)}) %all-gather.2.cloned.1.call-update) | async-done | bytes 1757200 | tf_op jit(solution)/shard_map/all_gather | solution.py:57
  55.6 1.9 %reshape.53 = bf16[3,286,1024]{2,1,0:T(8,128)(2,1)S(1)} reshape(bf16[858,1024]{1,0:T(8,128)(2,1)} %all-gather.2.cloned.1.call-done) | data formatting | bytes 3514368 | tf_op jit(solution)/shard_map/reshape | solution.py:63
  57.5 0.0 copy-start.4
  57.5 1.8 %fusion = f32[8,286,1024]{2,0,1:T(8,128)S(1)} fusion(bf16[3,286,1024]{2,1,0:T(8,128)(2,1)S(1)} %reshape.53, s32[8]{0:T(128)S(1)} %and_select_fusion), kind=kOutput, calls=%fused_computation.1 | convolution fusion | flops 14057496 | bytes 11128864 | tf_op jit(solution)/shard_map/oc,cix->oix/dot_general | solution.py:62
  59.3 0.9 copy-done.4
  60.2 5.4 %multiply_reduce_fusion = f32[8,1024]{1,0:T(8,128)S(1)} fusion(f32[8,286,1024]{2,0,1:T(8,128)S(1)} %fusion, bf16[8,286,858]{2,0,1:T(8,128)(2,1)S(1)} %copy-done.4, bf16[858,1024]{1,0:T(8,128)(2,1)S(1)} %copy-done.1), kind=kOutput, calls=%fused_computation | convolution fusion | flops 4025114624 | bytes 15087808 | tf_op jit(solution)/shard_map/dot_general | solution.py:59
  65.6 0.0 copy-start.2
  65.6 0.6 convert_bitcast_fusion
  66.2 6.2 %all-to-all-start = ((bf16[8,8,128]{2,0,1:T(8,128)(2,1)}), bf16[8,8,128]{2,0,1:T(8,128)(2,1)S(1)}, u32[]{:S(2)}, u32[]{:S(2)}) async-start(bf16[8,8,128]{2,0,1:T(8,128)(2,1)} %convert_bitcast_fusion), calls=%async_computation | async-start | bytes 32768 | tf_op jit(solution)/shard_map/all_to_all | solution.py:68
  72.4 0.1 fusion.6
  72.5 0.2 copy.13
  72.7 7.4 %all-to-all-done = bf16[8,8,128]{2,0,1:T(8,128)(2,1)S(1)} async-done(((bf16[8,8,128]{2,0,1:T(8,128)(2,1)}), bf16[8,8,128]{2,0,1:T(8,128)(2,1)S(1)}, u32[]{:S(2)}, u32[]{:S(2)}) %all-to-all-start) | async-done | bytes 16416 | tf_op jit(solution)/shard_map/all_to_all | solution.py:68
  80.2 1.0 %fusion.3 = f32[858,128]{1,0:T(8,128)} fusion(f32[858,128]{1,0:T(8,128)S(1)} %copy-done, f32[858,128]{1,0:T(8,128)S(1)} %mul.109, s32[64]{0:T(128)S(1)} %copy-done.3, bf16[8,8,128]{2,0,1:T(8,128)(2,1)S(1)} %all-to-all-done), kind=kOutput, calls=%fused_computation.6 | convolution fusion | flops 14441856 | bytes 1334528 | tf_op jit(solution)/shard_map/dot_general | solution.py:72
  (8 shorter events, 0.0 us)
Async XLA Ops:
  7.2 48.4 %all-gather.2.cloned.1.call-start = ((), (), s32[]{:S(2)}) async-start(), calls=%async_computation.1 | async-start | bytes 1990656 | tf_op jit(solution)/shard_map/all_gather | solution.py:57
  10.3 21.1 %collective-permute-start = (f32[858,1]{1,0:T(8,128)S(1)}, f32[858,1]{1,0:T(8,128)S(1)}, u32[]{:S(2)}, u32[]{:S(2)}) collective-permute-start(f32[858,1]{1,0:T(8,128)S(1)} %get-tuple-element.9), channel_id=1, source_target_pairs={{0,1},{1,2},{2,3},{3,4},{4,5},{5,6},{6,7},{7,8},{8,9},{9,10},{10,1... | collective-permute-start | bytes 10304 | tf_op jit(solution)/shard_map/ppermute | solution.py:20
  12.2 20.6 %collective-permute-start.1 = (f32[858,1]{1,0:T(8,128)S(1)}, f32[858,1]{1,0:T(8,128)S(1)}, u32[]{:S(2)}, u32[]{:S(2)}) collective-permute-start(f32[858,1]{1,0:T(8,128)S(1)} %get-tuple-element.10), channel_id=1, source_target_pairs={{1,0},{2,1},{3,2},{4,3},{5,4},{6,5},{7,6},{8,7},{9,8},{10,9},{11,1... | collective-permute-start | bytes 10304 | tf_op jit(solution)/shard_map/ppermute | solution.py:21
  57.5 1.8 %copy-start.1 = (bf16[858,1024]{1,0:T(8,128)(2,1)S(1)}, bf16[858,1024]{1,0:T(8,128)(2,1)}, u32[]{:S(2)}) copy-start(bf16[858,1024]{1,0:T(8,128)(2,1)} %all-gather.2.cloned.1.call-done) | copy-start | bytes 5271556
  57.5 2.7 %copy-start.4 = (bf16[8,286,858]{2,0,1:T(8,128)(2,1)S(1)}, bf16[8,286,858]{2,0,1:T(8,128)(2,1)}, u32[]{:S(2)}) copy-start(bf16[8,286,858]{2,0,1:T(8,128)(2,1)} %param.6) | copy-start | bytes 11778628
  60.2 20.0 %copy-start = (f32[858,128]{1,0:T(8,128)S(1)}, f32[858,128]{1,0:T(8,128)}, u32[]{:S(2)}) copy-start(f32[858,128]{1,0:T(8,128)} %param.5) | copy-start | bytes 1317892
  60.2 20.0 %copy-start.3 = (s32[64]{0:T(128)S(1)}, s32[64]{0:T(128)}, u32[]{:S(2)}) copy-start(s32[64]{0:T(128)} %param.9) | copy-start | bytes 772
  65.6 15.6 %copy-start.2 = (f32[8,1024]{1,0:T(8,128)}, f32[8,1024]{1,0:T(8,128)S(1)}, u32[]{:S(2)}) copy-start(f32[8,1024]{1,0:T(8,128)S(1)} %multiply_reduce_fusion) | copy-start | bytes 98308
  66.2 14.0 %all-to-all-start = ((bf16[8,8,128]{2,0,1:T(8,128)(2,1)}), bf16[8,8,128]{2,0,1:T(8,128)(2,1)S(1)}, u32[]{:S(2)}, u32[]{:S(2)}) async-start(bf16[8,8,128]{2,0,1:T(8,128)(2,1)} %convert_bitcast_fusion), calls=%async_computation | async-start | bytes 32768 | tf_op jit(solution)/shard_map/all_to_all | solution.py:68
Sparse Core Ops, SparseCore 0:
  10.7 44.8 all-gather.1
where the time goes:
time: 88.5 us; the launch traced here: 88 us
  waiting for transfers between devices  28.3 us (32%)
  starting transfers between devices  21.4 us (24%)
  between operations  14.2 us (16%)
  matrix products  11.8 us (13%)
  other arithmetic  6.99 us (8%)
  local copies, waits for them, and re-layouts  5.42 us (6%)
    all_gather x1, waiting for transfers between devices, shards(): lax.all_gather(state.astype(jnp.bfloat16), 'mode', axis=1, tiled=True)  16.5 us
    ppermute x1, starting transfers between devices, extended_2(): after = lax.ppermute(first, axis, down)  13.3 us
    all_to_all x1, waiting for transfers between devices, shards(): lax.all_to_all(collision.astype(jnp.bfloat16), 'mode', split_axis=1, conc...  7.44 us
    all_to_all x1, starting transfers between devices, shards(): lax.all_to_all(collision.astype(jnp.bfloat16), 'mode', split_axis=1, conc...  6.19 us
    dot_general x1, matrix products, shards(): jnp.dot(flat, piece, preferred_element_type=jnp.float32)  5.41 us
    dot_general x1, matrix products, upwind_transport(): jnp.einsum('ab,cbx->cax', matrix, blocks, precision=lax.Precision.HIGHEST)  3.58 us
    ppermute x1, waiting for transfers between devices, extended_2(): before = lax.ppermute(last, axis, up)  2.96 us
    ppermute x1, starting transfers between devices, extended_2(): before = lax.ppermute(last, axis, up)  1.92 us
  transfers between devices with their start and end apart: 4, of which 4 were waited for; matrix products, arithmetic and copies ran while one was open for 12% of the time, Pallas kernels for 0%

commit v1 on v0

--- a/solution.py
+++ b/solution.py
@@ -2,6 +2,7 @@
 import jax.numpy as jnp
 from jax import lax
 from jax.sharding import PartitionSpec as P
+from jax.lax import all_to_all, axis_size
 
 CLASSES = 3
 MODES = 286
@@ -54,7 +55,12 @@
     )
     flat = tensor.reshape(per_device * MODES, CLASSES * MODES)
     matrix = advection_matrix(table)
-    piece = lax.all_gather(state.astype(jnp.bfloat16), "mode", axis=1, tiled=True)
+    piece = jnp.concatenate(
+        all_to_all(
+            jnp.stack(axis_size("mode") * [state.astype(jnp.bfloat16)], axis=0), "mode", 0, 0
+        ),
+        axis=1,
+    )
     width = piece.shape[1]
     product = jnp.dot(flat, piece, preferred_element_type=jnp.float32).reshape(
         per_device, MODES, width

time: 88.5 us -> 115 us (1.30)
  the two profiles are of different devices: /device:TPU:4 before, /device:TPU:96 now
where the time goes in v1:
time: 115 us; the launch traced here: 114 us
  waiting for transfers between devices  51.4 us (45%)
  starting transfers between devices  21.3 us (19%)
  local copies, waits for them, and re-layouts  17 us (15%)
  matrix products  13.4 us (12%)
  other arithmetic  10.1 us (9%)
    ppermute x1, waiting for transfers between devices, extended_2(): before = lax.ppermute(last, axis, up)  44 us
    all_to_all x1, starting transfers between devices, shards(): all_to_all(jnp.stack(axis_size('mode') * [state.astype(jnp.bfloat16)], ax...  9.41 us
    all_to_all x1, waiting for transfers between devices, shards(): lax.all_to_all(collision.astype(jnp.bfloat16), 'mode', split_axis=1, conc...  7.36 us
    ppermute x1, starting transfers between devices, extended_2(): after = lax.ppermute(first, axis, down)  6.16 us
    unnamed x22, local copies, waits for them, and re-layouts  5.97 us
    dot_general x1, matrix products, shards(): jnp.dot(flat, piece, preferred_element_type=jnp.float32)  5.45 us
    reshape x2, local copies, waits for them, and re-layouts, shards(): jnp.concatenate(all_to_all(jnp.stack(axis_size('mode') * [state.astype(jn...  4.12 us
    dot_general x1, matrix products, upwind_transport(): jnp.einsum('ab,cbx->cax', matrix, blocks, precision=lax.Precision.HIGHEST)  3.57 us
  transfers between devices with their start and end apart: 4, of which 2 were waited for; matrix products, arithmetic and copies ran while one was open for 17% of the time, Pallas kernels for 0%

profile of v1, /device:TPU:96, one launch (start us, length us, event | category | flops | bytes accessed | tf_op | source)
XLA Modules:
  0.0 114.0 jit_solution(9065194865861547311)
XLA Ops:
  0.6 1.0 convert_element_type.22
  1.7 1.5 %stack.2 = bf16[8,858,128]{2,1,0:T(8,128)(2,1)} broadcast(bf16[858,128]{1,0:T(8,128)(2,1)S(1)} %convert_element_type.22), dimensions={1,2} | broadcast | bytes 1976832 | tf_op jit(solution)/shard_map/stack | solution.py:60
  3.1 9.4 %all-to-all-start = ((bf16[8,858,128]{2,1,0:T(8,128)(2,1)}), bf16[8,858,128]{2,1,0:T(8,128)(2,1)S(1)}, u32[]{:S(2)}, u32[]{:S(2)}) async-start(bf16[8,858,128]{2,1,0:T(8,128)(2,1)} %stack.2), calls=%async_computation | async-start | bytes 3538944 | tf_op jit(solution)/shard_map/all_to_all | solution.py:59
  12.6 0.2 fusion.25
  12.7 2.4 %collective-permute-start = (f32[858,1]{1,0:T(8,128)S(1)}, f32[858,1]{1,0:T(8,128)S(1)}, u32[]{:S(2)}, u32[]{:S(2)}) collective-permute-start(f32[858,1]{1,0:T(8,128)S(1)} %get-tuple-element.9), channel_id=1, source_target_pairs={{0,1},{1,2},{2,3},{3,4},{4,5},{5,6},{6,7},{7,8},{8,9},{9,10},{10,1... | collective-permute-start | bytes 10304 | tf_op jit(solution)/shard_map/ppermute | solution.py:21
  15.2 6.2 %collective-permute-start.1 = (f32[858,1]{1,0:T(8,128)S(1)}, f32[858,1]{1,0:T(8,128)}, u32[]{:S(2)}, u32[]{:S(2)}) collective-permute-start(f32[858,1]{1,0:T(8,128)S(1)} %get-tuple-element.10), channel_id=1, source_target_pairs={{1,0},{2,1},{3,2},{4,3},{5,4},{6,5},{7,6},{8,7},{9,8},{10,9},{11,1... | collective-permute-start | bytes 10304 | tf_op jit(solution)/shard_map/ppermute | solution.py:22
  21.3 0.7 sqrt_reduce_fusion.1
  22.1 1.4 %add_reduce_fusion.1 = (s32[286]{0:T(512)S(1)}, s32[286]{0:T(512)S(1)}, s32[286]{0:T(512)}) fusion(s32[286,3]{0,1:T(4,128)} %param.7), kind=kLoop, calls=%fused_computation.34 | loop fusion | flops 1716 | bytes 6864 | tf_op jit(solution)/shard_map/sub | solution.py:30
  23.5 1.2 %broadcast_multiply_fusion.1 = (f32[3]{0:T(128)}, f32[3]{0:T(128)}) fusion(f32[3]{0:T(128)} %param.8), kind=kLoop, calls=%fused_computation.38 | loop fusion | flops 6 | bytes 36 | tf_op jit(solution)/shard_map/mul | solution.py:41
  24.6 1.2 %and_select_fusion = s32[8]{0:T(128)} fusion(s32[64]{0:T(128)} %param.9, s32[]{:T(128)S(6)} %select_n.8), kind=kLoop, calls=%fused_computation.30 | loop fusion | flops 64 | bytes 68 | tf_op jit(solution)/shard_map/jit(floor_divide)/jit(_where)/select_n | solution.py:53
  25.9 44.0 %collective-permute-done = f32[858,1]{1,0:T(8,128)S(1)} collective-permute-done((f32[858,1]{1,0:T(8,128)S(1)}, f32[858,1]{1,0:T(8,128)S(1)}, u32[]{:S(2)}, u32[]{:S(2)}) %collective-permute-start) | collective-permute-done | bytes 3464 | tf_op jit(solution)/shard_map/ppermute | solution.py:21
  69.9 2.3 %pad_maximum_fusion = f32[858,130]{1,0:T(8,128)} fusion(f32[858,1]{1,0:T(8,128)} %collective-permute-done.1, f32[858,128]{1,0:T(8,128)S(1)} %copy-done, f32[858,1]{1,0:T(8,128)S(1)} %collective-permute-done), kind=kLoop, calls=%fused_computation.6 | loop fusion | flops 223080 | bytes 892320 | tf_op jit(solution)/shard_map/concatenate | solution.py:23
  72.2 1.3 %reshape.64 = f32[3,286,130]{2,1,0:T(8,128)S(1)} reshape(f32[858,130]{1,0:T(8,128)} %pad_maximum_fusion) | data formatting | bytes 892320 | tf_op jit(solution)/shard_map/reshape | solution.py:36
  73.5 1.5 %fusion.24 = (f32[3,286,129]{2,1,0:T(8,128)}, f32[3,286,129]{2,1,0:T(8,128)}) fusion(f32[3,286,130]{2,1,0:T(8,128)S(1)} %reshape.64), kind=kLoop, calls=%fused_computation.40 | loop fusion | bytes 1770912 | tf_op jit(solution)/shard_map/slice | solution.py:43
  75.0 2.4 %copy.31 = f32[3,286,129]{1,2,0:T(8,128)} copy(f32[3,286,129]{2,1,0:T(8,128)} %get-tuple-element.8) | data formatting | bytes 885456
  77.4 2.3 %copy.32 = f32[3,286,129]{1,2,0:T(8,128)} copy(f32[3,286,129]{2,1,0:T(8,128)} %get-tuple-element.7) | data formatting | bytes 885456
  79.7 3.6 %convolution_bitcast_fusion = f32[3,286,130]{1,2,0:T(8,128)S(1)} fusion(f32[3,286,130]{2,1,0:T(8,128)S(1)} %reshape.64, f32[286]{0:T(512)S(1)} %get-tuple-element.3, f32[286]{0:T(512)S(1)} %get-tuple-element.2, s32[286]{0:T(512)S(1)} %copy-done.4, s32[286]{0:T(512)S(1)} %get-tuple-element.5, s32[286]{0:T(512)S(1)} %get-tuple-element.4), kind=kOutput, calls=%fused_computation.3 | convolution fusion | flops 383214272 | bytes 898040 | tf_op jit(solution)/shard_map/ab,cbx->cax/dot_general | solution.py:37
  83.3 1.5 %fusion.4 = f32[3,286,129]{1,2,0:T(8,128)S(1)} fusion(f32[3,286,130]{1,2,0:T(8,128)S(1)} %convolution_bitcast_fusion, f32[3,286,129]{1,2,0:T(8,128)} %copy.31, f32[3,286,129]{1,2,0:T(8,128)} %copy.32, f32[3]{0:T(128)S(1)} %copy-done.8, f32[3]{0:T(128)S(1)} %copy-done.7), kind=kLoop, calls=%fused_computation.9 | loop fusion | flops 553410 | bytes 2213664 | tf_op jit(solution)/shard_map/sub | solution.py:41
  84.8 1.2 %copy-done.1 = bf16[8,858,128]{2,1,0:T(8,128)(2,1)} copy-done((bf16[8,858,128]{2,1,0:T(8,128)(2,1)}, bf16[8,858,128]{2,1,0:T(8,128)(2,1)S(1)}, u32[]{:S(2)}) %copy-start.1) | copy-done | bytes 1757208
  86.0 2.2 %copy.22 = bf16[858,8,128]{2,1,0:T(8,128)(2,1)S(1)} copy(bf16[858,8,128]{2,0,1:T(8,128)(2,1)} %bitcast.19) | data formatting | bytes 3514368 | tf_op jit(solution)/shard_map/reshape | solution.py:58
  88.2 2.3 %reshape_reshape.3 = bf16[3,286,1024]{2,1,0:T(8,128)(2,1)} reshape(bf16[858,8,128]{2,1,0:T(8,128)(2,1)S(1)} %copy.22) | data formatting | bytes 3514368 | tf_op jit(solution)/shard_map/reshape;reshape | solution.py:69
  90.4 2.0 %reshape.62 = bf16[858,1024,1]{1,0,2:T(8,128)(2,1)} reshape(bf16[858,8,128]{2,1,0:T(8,128)(2,1)S(1)} %copy.22) | data formatting | bytes 3514368 | tf_op jit(solution)/shard_map/reshape | solution.py:58
  92.4 3.4 %fusion = f32[8,286,1024]{2,0,1:T(8,128)S(1)} fusion(bf16[3,286,1024]{2,1,0:T(8,128)(2,1)} %reshape_reshape.3, s32[8]{0:T(128)S(1)} %copy-done.6), kind=kOutput, calls=%fused_computation.1 | convolution fusion | flops 14057496 | bytes 11128864 | tf_op jit(solution)/shard_map/oc,cix->oix/dot_general | solution.py:68
  95.9 5.5 %multiply_reduce_fusion = f32[8,1024]{1,0:T(8,128)S(1)} fusion(f32[8,286,1024]{2,0,1:T(8,128)S(1)} %fusion, bf16[8,286,858]{2,0,1:T(8,128)(2,1)S(1)} %copy-done.9, bf16[858,1024,1]{1,0,2:T(8,128)(2,1)S(1)} %copy-done.2), kind=kOutput, calls=%fused_computation | convolution fusion | flops 4025114624 | bytes 15087808 | tf_op jit(solution)/shard_map/dot_general | solution.py:65
  101.3 0.0 copy-start.3
  101.3 0.0 copy-start.5
  101.3 0.6 convert_bitcast_fusion
  102.0 3.3 %all-to-all-start.1 = ((bf16[8,8,128]{2,0,1:T(8,128)(2,1)}), bf16[8,8,128]{2,0,1:T(8,128)(2,1)S(1)}, u32[]{:S(2)}, u32[]{:S(2)}) async-start(bf16[8,8,128]{2,0,1:T(8,128)(2,1)} %convert_bitcast_fusion), calls=%async_computation.1 | async-start | bytes 32768 | tf_op jit(solution)/shard_map/all_to_all | solution.py:74
  105.3 0.1 fusion.5
  105.4 0.2 copy.21
  105.6 7.4 %all-to-all-done.1 = bf16[8,8,128]{2,0,1:T(8,128)(2,1)S(1)} async-done(((bf16[8,8,128]{2,0,1:T(8,128)(2,1)}), bf16[8,8,128]{2,0,1:T(8,128)(2,1)S(1)}, u32[]{:S(2)}, u32[]{:S(2)}) %all-to-all-start.1) | async-done | bytes 16416 | tf_op jit(solution)/shard_map/all_to_all | solution.py:74
  113.0 1.0 fusion.2
  (20 shorter events, 0.1 us)
Async XLA Ops:
  1.7 10.9 %copy-start = (f32[858,128]{1,0:T(8,128)S(1)}, f32[858,128]{1,0:T(8,128)}, u32[]{:S(2)}) copy-start(f32[858,128]{1,0:T(8,128)} %param.5) | copy-start | bytes 1317892
  3.1 81.6 %all-to-all-start = ((bf16[8,858,128]{2,1,0:T(8,128)(2,1)}), bf16[8,858,128]{2,1,0:T(8,128)(2,1)S(1)}, u32[]{:S(2)}, u32[]{:S(2)}) async-start(bf16[8,858,128]{2,1,0:T(8,128)(2,1)} %stack.2), calls=%async_computation | async-start | bytes 3538944 | tf_op jit(solution)/shard_map/all_to_all | solution.py:59
  12.7 57.1 %collective-permute-start = (f32[858,1]{1,0:T(8,128)S(1)}, f32[858,1]{1,0:T(8,128)S(1)}, u32[]{:S(2)}, u32[]{:S(2)}) collective-permute-start(f32[858,1]{1,0:T(8,128)S(1)} %get-tuple-element.9), channel_id=1, source_target_pairs={{0,1},{1,2},{2,3},{3,4},{4,5},{5,6},{6,7},{7,8},{8,9},{9,10},{10,1... | collective-permute-start | bytes 10304 | tf_op jit(solution)/shard_map/ppermute | solution.py:21
  15.2 54.7 %collective-permute-start.1 = (f32[858,1]{1,0:T(8,128)S(1)}, f32[858,1]{1,0:T(8,128)}, u32[]{:S(2)}, u32[]{:S(2)}) collective-permute-start(f32[858,1]{1,0:T(8,128)S(1)} %get-tuple-element.10), channel_id=1, source_target_pairs={{1,0},{2,1},{3,2},{4,3},{5,4},{6,5},{7,6},{8,7},{9,8},{10,9},{11,1... | collective-permute-start | bytes 10304 | tf_op jit(solution)/shard_map/ppermute | solution.py:22
  75.0 4.7 %copy-start.4 = (s32[286]{0:T(512)S(1)}, s32[286]{0:T(512)}, u32[]{:S(2)}) copy-start(s32[286]{0:T(512)} %get-tuple-element.6) | copy-start | bytes 3436
  75.0 8.3 %copy-start.7 = (f32[3]{0:T(128)S(1)}, f32[3]{0:T(128)}, u32[]{:S(2)}) copy-start(f32[3]{0:T(128)} %get-tuple-element.11) | copy-start | bytes 40
  75.0 8.3 %copy-start.8 = (f32[3]{0:T(128)S(1)}, f32[3]{0:T(128)}, u32[]{:S(2)}) copy-start(f32[3]{0:T(128)} %get-tuple-element.12) | copy-start | bytes 40
  84.8 1.2 %copy-start.1 = (bf16[8,858,128]{2,1,0:T(8,128)(2,1)}, bf16[8,858,128]{2,1,0:T(8,128)(2,1)S(1)}, u32[]{:S(2)}) copy-start(bf16[8,858,128]{2,1,0:T(8,128)(2,1)S(1)} %all-to-all-done) | copy-start | bytes 5271556
  90.4 2.0 %copy-start.6 = (s32[8]{0:T(128)S(1)}, s32[8]{0:T(128)}, u32[]{:S(2)}) copy-start(s32[8]{0:T(128)} %and_select_fusion) | copy-start | bytes 100
  92.4 3.4 %copy-start.2 = (bf16[858,1024,1]{1,0,2:T(8,128)(2,1)S(1)}, bf16[858,1024,1]{1,0,2:T(8,128)(2,1)}, u32[]{:S(2)}) copy-start(bf16[858,1024,1]{1,0,2:T(8,128)(2,1)} %reshape.62) | copy-start | bytes 5271556
  92.4 3.4 %copy-start.9 = (bf16[8,286,858]{2,0,1:T(8,128)(2,1)S(1)}, bf16[8,286,858]{2,0,1:T(8,128)(2,1)}, u32[]{:S(2)}) copy-start(bf16[8,286,858]{2,0,1:T(8,128)(2,1)} %param.6) | copy-start | bytes 11778628
  101.3 12.7 %copy-start.3 = (f32[8,1024]{1,0:T(8,128)}, f32[8,1024]{1,0:T(8,128)S(1)}, u32[]{:S(2)}) copy-start(f32[8,1024]{1,0:T(8,128)S(1)} %multiply_reduce_fusion) | copy-start | bytes 98308
  101.3 11.7 %copy-start.5 = (s32[64]{0:T(128)S(1)}, s32[64]{0:T(128)}, u32[]{:S(2)}) copy-start(s32[64]{0:T(128)} %param.9) | copy-start | bytes 772
  102.0 11.0 %all-to-all-start.1 = ((bf16[8,8,128]{2,0,1:T(8,128)(2,1)}), bf16[8,8,128]{2,0,1:T(8,128)(2,1)S(1)}, u32[]{:S(2)}, u32[]{:S(2)}) async-start(bf16[8,8,128]{2,0,1:T(8,128)(2,1)} %convert_bitcast_fusion), calls=%async_computation.1 | async-start | bytes 32768 | tf_op jit(solution)/shard_map/all_to_all | solution.py:74
